TPU v7x, 256 devices: a whole 4x4x8 slice. The times are simulated.
256 devices in a mesh: section: 2 (over core), blk: 128 (over z, x, y).
Axes of the slice: x: 4, y: 4, z: 8, core: 2. Of those that a mesh axis runs over, the one named last changes fastest.
Arguments:
- hidden: bfloat16 [2, 384, 3072], P(None, 'blk'), may hold values from -4 to 4
- qkv_weight: bfloat16 [2, 3072, 9216], P('section', None, 'blk'), may hold values from -0.109375 to 0.109375
- out_weight: bfloat16 [2, 3072, 3072], P('section', None, 'blk'), may hold values from -0.109375 to 0.109375
- modulation: float32 [2, 50, 3, 3072], P('section'), may hold values from -3 to 3
- timestep: int32 [1], replicated, may hold values from 0 to 49
- fresh: int32 [2, 2, 128], P('section'), may hold values 0 or 1
- live: int32 [2, 128], replicated, may hold values from 0 to 1, as said below
- k_stale: bfloat16 [2, 2, 384, 3072], P('section', None, 'blk'), may hold values from -6 to 6
- v_stale: bfloat16 [2, 2, 384, 3072], P('section', None, 'blk'), may hold values from -16 to 16
Outputs:
- layer_outputs: bfloat16 [2, 2, 384, 3072], P('section', None, 'blk')
Inputs may be any that keep to these rules, and one draw needn't show every extreme that they name: Block 0 of every request is live.
All inputs are finite; a program needn't handle non-finite values. No bound on the sum of `fresh` on one device may be relied on, other than what follows from the above.
Results may differ from a plain program's by a relative error of at most 0.017.
Values may be sent and summed in bfloat16 or wider, within the bound.
A program may use at most 64 MiB of HBM per device.

v0:
```python
import jax
import jax.numpy as jnp
from jax import lax
from jax.sharding import PartitionSpec as P


def from_behind(shard, axis, by):
    count = lax.axis_size(axis)
    pairs = [(i, i + by) for i in range(count) if 0 <= i + by < count]
    return lax.ppermute(shard, axis, pairs)


def attend(layer_in, qkv_cols, out_cols, modulate, fresh_own, old_keys, old_values, live):
    stream = layer_in.astype(jnp.float32)
    center = jnp.mean(stream, axis=-1, keepdims=True)
    variance = jnp.mean((stream - center) ** 2, axis=-1, keepdims=True)
    normed = (stream - center) / jnp.sqrt(variance + 1e-06) * (1.0 + modulate[0]) + modulate[1]
    normed_b = normed.astype(jnp.bfloat16)
    columns = jnp.einsum(
        "rnd,dc->rnc",
        lax.all_gather(normed_b, "blk", axis=1, tiled=True),
        qkv_cols,
        preferred_element_type=jnp.float32,
    ).astype(jnp.bfloat16)
    projected = lax.all_to_all(columns, "blk", split_axis=1, concat_axis=2, tiled=True)
    num_req, num_rows, width = layer_in.shape
    queries = projected[:, :, :width]
    new_keys = projected[:, :, width : 2 * width]
    new_values = projected[:, :, 2 * width :]
    use_fresh = (fresh_own == 1)[:, None, None]
    keys = jnp.where(use_fresh, new_keys, old_keys)
    values = jnp.where(use_fresh, new_values, old_values)
    num_heads = width // 64
    num_blocks = live.shape[1]
    q_heads = queries.reshape(num_req, num_rows, num_heads, 64)
    live_float = live.astype(jnp.float32)
    run_max = jnp.full((num_req, num_heads, num_rows), -1e30, jnp.float32)
    key_piece = lax.all_gather(keys, "blk", axis=1, tiled=True)
    value_piece = lax.all_gather(values, "blk", axis=1, tiled=True)
    piece_rows = key_piece.shape[1]
    key_heads = key_piece.reshape(num_req, piece_rows, num_heads, 64)
    value_heads = value_piece.reshape(num_req, piece_rows, num_heads, 64)
    scores = (
        jnp.einsum("qrhd,qnhd->qhrn", q_heads, key_heads, preferred_element_type=jnp.float32)
        * 0.125
    )
    block_ids = jnp.arange(piece_rows) // num_rows
    one_hot = (block_ids[:, None] == jnp.arange(num_blocks)[None, :]).astype(jnp.float32)
    usable = jnp.einsum("qb,nb->qn", live_float, one_hot) > 0.5
    usable = usable[:, None, None, :]
    scores = jnp.where(usable, scores, -1e30)
    new_max = jnp.maximum(run_max, jnp.max(scores, axis=-1))
    weights = jnp.where(usable, jnp.exp(scores - new_max[..., None]), 0.0)
    new_sum = jnp.sum(weights, axis=-1)
    new_acc = jnp.einsum(
        "qhrn,qnhd->qhrd", weights, value_heads.astype(jnp.float32), precision=lax.Precision.HIGHEST
    )
    attn = new_acc / new_sum[..., None]
    attn = jnp.transpose(attn, (0, 2, 1, 3)).reshape(num_req, num_rows, width).astype(jnp.bfloat16)
    out_part = jnp.einsum(
        "rnd,dc->rnc",
        lax.all_gather(attn, "blk", axis=1, tiled=True),
        out_cols,
        preferred_element_type=jnp.float32,
    ).astype(jnp.bfloat16)
    mixed_back = lax.all_to_all(out_part, "blk", split_axis=1, concat_axis=2, tiled=True)
    return (stream + modulate[2] * mixed_back.astype(jnp.float32)).astype(jnp.bfloat16)


def pick_request(array, req_idx):
    return lax.dynamic_index_in_dim(array, req_idx, 0, keepdims=True)


def per_device(hidden, qkv_weight, out_weight, modulation, timestep, fresh, live, k_stale, v_stale):
    section_idx = lax.axis_index("section")
    block_idx = lax.axis_index("blk")
    steps_all = modulation.shape[1]
    pick_row = (jnp.arange(steps_all) == timestep[0]).astype(jnp.float32)
    modulate = jnp.einsum("t,tcd->cd", pick_row, modulation[0], precision=lax.Precision.HIGHEST)
    num_blocks = fresh.shape[2]
    own_column = (jnp.arange(num_blocks) == block_idx).astype(jnp.int32)
    fresh_own = jnp.sum(fresh[0] * own_column[None, :], axis=1)
    qkv_cols = qkv_weight[0]
    out_cols = out_weight[0]
    old_keys = k_stale[0]
    old_values = v_stale[0]
    num_req = hidden.shape[0]
    received = jnp.zeros_like(hidden[0:1])
    first_out = []
    second_out = []
    for tick_idx in range(num_req + 1):
        if tick_idx < num_req:
            own_input = hidden[tick_idx : tick_idx + 1]
        else:
            own_input = jnp.zeros_like(hidden[0:1])
        layer_in = jnp.where(section_idx == 0, own_input, received)
        req_idx = jnp.clip(tick_idx - section_idx, 0, num_req - 1)
        layer_out = attend(
            layer_in,
            qkv_cols,
            out_cols,
            modulate,
            pick_request(fresh_own, req_idx),
            pick_request(old_keys, req_idx),
            pick_request(old_values, req_idx),
            pick_request(live, req_idx),
        )
        if tick_idx < num_req:
            first_out.append(layer_out)
            received = from_behind(layer_out, "section", 1)
        if tick_idx >= 1:
            second_out.append(layer_out)
    result = jnp.where(
        section_idx == 0, jnp.concatenate(first_out, axis=0), jnp.concatenate(second_out, axis=0)
    )
    return result[None]


def solution(mesh):
    return jax.shard_map(
        per_device,
        mesh=mesh,
        in_specs=(
            P(None, "blk", None),
            P("section", None, "blk"),
            P("section", None, "blk"),
            P("section", None, None, None),
            P(),
            P("section", None, None),
            P(),
            P("section", None, "blk", None),
            P("section", None, "blk", None),
        ),
        out_specs=P("section", None, "blk", None),
        check_vma=False,
    )
```

profile of v0, /device:TPU:2, one launch (start us, length us, event | category | flops | bytes accessed | tf_op | source)
XLA Modules:
  0.0 1597.2 jit_solution(17317601868942555664)
XLA Ops:
  6.6 1.0 fusion.114
  7.6 1.0 multiply_reduce_fusion.2
  9.2 2.4 fusion.18
  11.7 0.7 add_convert_fusion.5
  12.8 120.3 %all-gather.13.cloned.1.call-done = bf16[1,384,3072]{2,0,1:T(2,128)(2,1)} async-done(((bf16[1,3,3072]{2,0,1:T(2,128)(2,1)}), bf16[1,384,3072]{2,0,1:T(2,128)(2,1)}) %all-gather.13.cloned.1.call-update) | async-done | bytes 2359312 | tf_op jit(solution)/shard_map/all_gather | solution.py:21
  133.0 3.2 fusion.42
  136.3 0.8 copy.110
  137.1 9.1 all-to-all-start
  146.4 0.6 fusion.121
  147.7 11.1 all-to-all-done
  159.7 0.6 copy.112
  160.4 0.6 copy.115
  161.5 109.9 %all-gather.15.cloned.1.call-done = bf16[1,384,3072]{2,0,1:T(2,128)(2,1)} async-done(((bf16[1,3,3072]{2,0,1:T(2,128)(2,1)}), bf16[1,384,3072]{2,0,1:T(2,128)(2,1)}) %all-gather.15.cloned.1.call-update) | async-done | bytes 2359312 | tf_op jit(solution)/shard_map/all_gather | solution.py:38
  271.4 10.0 copy.113
  281.4 0.6 fusion.122
  282.3 107.0 %all-gather.17.cloned.1.call-done = bf16[1,384,3072]{2,0,1:T(2,128)(2,1)} async-done(((bf16[1,3,3072]{2,0,1:T(2,128)(2,1)}), bf16[1,384,3072]{2,0,1:T(2,128)(2,1)}) %all-gather.17.cloned.1.call-update) | async-done | bytes 2359312 | tf_op jit(solution)/shard_map/all_gather | solution.py:39
  389.2 10.0 copy.116
  399.2 2.6 fusion.47
  401.9 0.7 convert_element_type.264
  402.6 114.2 %all-gather.19.cloned.1.call-done = bf16[1,384,3072]{2,0,1:T(2,128)(2,1)} async-done(((bf16[1,3,3072]{2,0,1:T(2,128)(2,1)}), bf16[1,384,3072]{2,0,1:T(2,128)(2,1)}) %all-gather.19.cloned.1.call-update) | async-done | bytes 2359312 | tf_op jit(solution)/shard_map/all_gather | solution.py:62
  516.8 3.1 fusion.63
  520.1 21.4 %all_to_all.81 = bf16[1,384,24]{2,0,1:T(2,128)(2,1)S(1)} all-to-all(bf16[1,384,24]{2,0,1:T(2,128)(2,1)S(1)} %copy.119), channel_id=1, replica_groups=mesh['section'=2,'blk'=128] {'blk'}, dimensions={1} | all-to-all | bytes 36864 | tf_op jit(solution)/shard_map/all_to_all | solution.py:66
  542.0 1.3 collective-permute-start
  543.3 0.8 collective-permute-done
  544.5 0.7 add_convert_fusion.3
  545.3 111.1 %all-gather.21.cloned.1.call-done = bf16[1,384,3072]{2,0,1:T(2,128)(2,1)} async-done(((bf16[1,3,3072]{2,0,1:T(2,128)(2,1)}), bf16[1,384,3072]{2,0,1:T(2,128)(2,1)}) %all-gather.21.cloned.1.call-update) | async-done | bytes 2359312 | tf_op jit(solution)/shard_map/all_gather | solution.py:21
  656.5 3.2 fusion.39
  659.7 0.8 copy.121
  660.5 9.1 all-to-all-start.2
  670.2 11.9 all-to-all-done.2
  683.1 0.6 copy.123
  683.8 0.6 copy.126
  684.9 109.9 %all-gather.23.cloned.1.call-done = bf16[1,384,3072]{2,0,1:T(2,128)(2,1)} async-done(((bf16[1,3,3072]{2,0,1:T(2,128)(2,1)}), bf16[1,384,3072]{2,0,1:T(2,128)(2,1)}) %all-gather.23.cloned.1.call-update) | async-done | bytes 2359312 | tf_op jit(solution)/shard_map/all_gather | solution.py:38
  794.9 10.0 copy.124
  805.7 106.9 %all-gather.25.cloned.1.call-done = bf16[1,384,3072]{2,0,1:T(2,128)(2,1)} async-done(((bf16[1,3,3072]{2,0,1:T(2,128)(2,1)}), bf16[1,384,3072]{2,0,1:T(2,128)(2,1)}) %all-gather.25.cloned.1.call-update) | async-done | bytes 2359312 | tf_op jit(solution)/shard_map/all_gather | solution.py:39
  912.6 10.0 copy.127
  922.6 2.6 fusion.46
  925.2 0.7 convert_element_type.265
  926.0 114.2 %all-gather.27.cloned.1.call-done = bf16[1,384,3072]{2,0,1:T(2,128)(2,1)} async-done(((bf16[1,3,3072]{2,0,1:T(2,128)(2,1)}), bf16[1,384,3072]{2,0,1:T(2,128)(2,1)}) %all-gather.27.cloned.1.call-update) | async-done | bytes 2359312 | tf_op jit(solution)/shard_map/all_gather | solution.py:62
  1040.2 3.1 fusion.60
  1043.5 21.4 %all_to_all.82 = bf16[1,384,24]{2,0,1:T(2,128)(2,1)S(1)} all-to-all(bf16[1,384,24]{2,0,1:T(2,128)(2,1)S(1)} %copy.130), channel_id=1, replica_groups=mesh['section'=2,'blk'=128] {'blk'}, dimensions={1} | all-to-all | bytes 36864 | tf_op jit(solution)/shard_map/all_to_all | solution.py:66
  1065.4 1.5 collective-permute-start.1
  1066.9 0.6 collective-permute-done.1
  1067.9 0.7 add_convert_fusion.1
  1068.7 111.1 %all-gather.29.cloned.1.call-done = bf16[1,384,3072]{2,0,1:T(2,128)(2,1)} async-done(((bf16[1,3,3072]{2,0,1:T(2,128)(2,1)}), bf16[1,384,3072]{2,0,1:T(2,128)(2,1)}) %all-gather.29.cloned.1.call-update) | async-done | bytes 2359312 | tf_op jit(solution)/shard_map/all_gather | solution.py:21
  1179.8 3.2 fusion.36
  1183.0 0.8 copy.132
  1183.9 9.1 all-to-all-start.4
  1193.6 11.9 all-to-all-done.4
  1206.4 0.6 copy.134
  1207.1 0.6 copy.137
  1208.2 109.9 %all-gather.31.cloned.1.call-done = bf16[1,384,3072]{2,0,1:T(2,128)(2,1)} async-done(((bf16[1,3,3072]{2,0,1:T(2,128)(2,1)}), bf16[1,384,3072]{2,0,1:T(2,128)(2,1)}) %all-gather.31.cloned.1.call-update) | async-done | bytes 2359312 | tf_op jit(solution)/shard_map/all_gather | solution.py:38
  1318.2 10.0 copy.135
  1328.2 0.6 fusion.124
  1329.0 107.0 %all-gather.33.cloned.1.call-done = bf16[1,384,3072]{2,0,1:T(2,128)(2,1)} async-done(((bf16[1,3,3072]{2,0,1:T(2,128)(2,1)}), bf16[1,384,3072]{2,0,1:T(2,128)(2,1)}) %all-gather.33.cloned.1.call-update) | async-done | bytes 2359312 | tf_op jit(solution)/shard_map/all_gather | solution.py:39
  1436.0 10.0 copy.138
  1445.9 2.6 fusion.45
  1448.6 0.7 convert_element_type.266
  1449.3 114.2 %all-gather.35.cloned.1.call-done = bf16[1,384,3072]{2,0,1:T(2,128)(2,1)} async-done(((bf16[1,3,3072]{2,0,1:T(2,128)(2,1)}), bf16[1,384,3072]{2,0,1:T(2,128)(2,1)}) %all-gather.35.cloned.1.call-update) | async-done | bytes 2359312 | tf_op jit(solution)/shard_map/all_gather | solution.py:62
  1563.5 3.1 fusion.57
  1566.7 0.9 copy.141
  1567.5 9.1 all-to-all-start.5
  1576.6 12.5 all-to-all-done.5
  1589.7 0.6 copy.143
  (106 shorter events, 9.0 us)
Async XLA Ops:
  6.5 126.5 %copy-start = (bf16[1,3072,72]{1,2,0:T(8,128)(2,1)S(1)}, bf16[1,3072,72]{1,2,0:T(8,128)(2,1)}, u32[]{:S(2)}) copy-start(bf16[1,3072,72]{1,2,0:T(8,128)(2,1)} %param.10) | copy-start | bytes 1327108
  6.5 5.1 copy-start.1
  6.5 6.0 copy-start.3
  6.5 6.0 copy-start.2
  6.5 126.5 %all-gather.13.cloned.1.call-start = ((), (), s32[]{:S(2)}) async-start(), calls=%async_computation.6 | async-start | bytes 4755456 | tf_op jit(solution)/shard_map/all_gather | solution.py:21
  12.5 133.8 %copy-start.4 = (s32[1,2,128]{2,1,0:T(2,128)S(1)}, s32[1,2,128]{2,1,0:T(2,128)}, u32[]{:S(2)}) copy-start(s32[1,2,128]{2,1,0:T(2,128)} %param.14) | copy-start | bytes 3076
  12.8 148.4 %copy-start.6 = (s32[2,128]{1,0:T(2,128)S(1)}, s32[2,128]{1,0:T(2,128)}, u32[]{:S(2)}) copy-start(s32[2,128]{1,0:T(2,128)} %param.15) | copy-start | bytes 3076
  137.1 21.6 %all-to-all-start = ((bf16[1,384,72]{2,0,1:T(2,128)(2,1)}), bf16[1,384,72]{2,0,1:T(2,128)(2,1)S(1)}, u32[]{:S(2)}, u32[]{:S(2)}) async-start(bf16[1,384,72]{2,0,1:T(2,128)(2,1)} %copy.110), calls=%async_computation | async-start | bytes 393216 | tf_op jit(solution)/shard_map/all_to_all | solution.py:25
  146.2 125.2 %all-gather.15.cloned.1.call-start = ((), (), s32[]{:S(2)}) async-start(), calls=%async_computation.7 | async-start | bytes 4755456 | tf_op jit(solution)/shard_map/all_gather | solution.py:38
  160.4 228.9 %all-gather.17.cloned.1.call-start = ((), (), s32[]{:S(2)}) async-start(), calls=%async_computation.8 | async-start | bytes 4755456 | tf_op jit(solution)/shard_map/all_gather | solution.py:39
  161.1 355.7 %all-gather.19.cloned.1.call-start = ((), (), s32[]{:S(2)}) async-start(), calls=%async_computation.9 | async-start | bytes 4755456 | tf_op jit(solution)/shard_map/all_gather | solution.py:62
  399.2 117.6 %copy-start.5 = (bf16[1,3072,24]{1,2,0:T(8,128)(2,1)S(1)}, bf16[1,3072,24]{1,2,0:T(8,128)(2,1)}, u32[]{:S(2)}) copy-start(bf16[1,3072,24]{1,2,0:T(8,128)(2,1)} %param.11) | copy-start | bytes 442372
  402.6 253.9 %all-gather.21.cloned.1.call-start = ((), (), s32[]{:S(2)}) async-start(), calls=%async_computation.10 | async-start | bytes 4755456 | tf_op jit(solution)/shard_map/all_gather | solution.py:21
  542.0 2.1 collective-permute-start
  660.5 21.6 %all-to-all-start.2 = ((bf16[1,384,72]{2,0,1:T(2,128)(2,1)}), bf16[1,384,72]{2,0,1:T(2,128)(2,1)S(1)}, u32[]{:S(2)}, u32[]{:S(2)}) async-start(bf16[1,384,72]{2,0,1:T(2,128)(2,1)} %copy.121), calls=%async_computation.2 | async-start | bytes 393216 | tf_op jit(solution)/shard_map/all_to_all | solution.py:25
  669.6 125.2 %all-gather.23.cloned.1.call-start = ((), (), s32[]{:S(2)}) async-start(), calls=%async_computation.11 | async-start | bytes 4755456 | tf_op jit(solution)/shard_map/all_gather | solution.py:38
  683.8 228.9 %all-gather.25.cloned.1.call-start = ((), (), s32[]{:S(2)}) async-start(), calls=%async_computation.12 | async-start | bytes 4755456 | tf_op jit(solution)/shard_map/all_gather | solution.py:39
  684.5 355.7 %all-gather.27.cloned.1.call-start = ((), (), s32[]{:S(2)}) async-start(), calls=%async_computation.13 | async-start | bytes 4755456 | tf_op jit(solution)/shard_map/all_gather | solution.py:62
  926.0 253.8 %all-gather.29.cloned.1.call-start = ((), (), s32[]{:S(2)}) async-start(), calls=%async_computation.14 | async-start | bytes 4755456 | tf_op jit(solution)/shard_map/all_gather | solution.py:21
  1065.4 2.1 collective-permute-start.1
  1183.9 21.6 %all-to-all-start.4 = ((bf16[1,384,72]{2,0,1:T(2,128)(2,1)}), bf16[1,384,72]{2,0,1:T(2,128)(2,1)S(1)}, u32[]{:S(2)}, u32[]{:S(2)}) async-start(bf16[1,384,72]{2,0,1:T(2,128)(2,1)} %copy.132), calls=%async_computation.4 | async-start | bytes 393216 | tf_op jit(solution)/shard_map/all_to_all | solution.py:25
  1193.0 125.2 %all-gather.31.cloned.1.call-start = ((), (), s32[]{:S(2)}) async-start(), calls=%async_computation.15 | async-start | bytes 4755456 | tf_op jit(solution)/shard_map/all_gather | solution.py:38
  1207.1 228.9 %all-gather.33.cloned.1.call-start = ((), (), s32[]{:S(2)}) async-start(), calls=%async_computation.16 | async-start | bytes 4755456 | tf_op jit(solution)/shard_map/all_gather | solution.py:39
  1207.8 355.7 %all-gather.35.cloned.1.call-start = ((), (), s32[]{:S(2)}) async-start(), calls=%async_computation.17 | async-start | bytes 4755456 | tf_op jit(solution)/shard_map/all_gather | solution.py:62
  1567.5 21.6 %all-to-all-start.5 = ((bf16[1,384,24]{2,0,1:T(2,128)(2,1)}), bf16[1,384,24]{2,0,1:T(2,128)(2,1)S(1)}, u32[]{:S(2)}, u32[]{:S(2)}) async-start(bf16[1,384,24]{2,0,1:T(2,128)(2,1)} %copy.141), calls=%async_computation.5 | async-start | bytes 393216 | tf_op jit(solution)/shard_map/all_to_all | solution.py:66
Sparse Core Ops, SparseCore 0:
  12.6 120.4 all-gather.12
  160.5 110.9 all-gather.14
  275.1 114.0 all-gather.16
  402.7 114.0 all-gather.18
  545.4 110.9 all-gather.20
  683.9 110.9 all-gather.22
  798.5 114.0 all-gather.24
  926.1 114.0 all-gather.26
  1068.8 110.9 all-gather.28
  1207.2 110.9 all-gather.30
  1321.9 114.0 all-gather.32
  1449.4 114.0 all-gather.34
where the time goes:
time: 1600 us
  waiting for transfers between devices  1380 us (86%)
  local copies, waits for them, and re-layouts  72.8 us (5%)
  blocking collectives  42.8 us (3%)
  starting transfers between devices  39.6 us (2%)
  matrix products  31.9 us (2%)
  between operations  16.6 us (1%)
    all_gather x3, waiting for transfers between devices, attend(): lax.all_gather(attn, 'blk', axis=1, tiled=True)  343 us
    all_gather x3, waiting for transfers between devices, attend(): lax.all_gather(normed_b, 'blk', axis=1, tiled=True)  343 us
    all_gather x3, waiting for transfers between devices, attend(): key_piece = lax.all_gather(keys, 'blk', axis=1, tiled=True)  330 us
    all_gather x3, waiting for transfers between devices, attend(): value_piece = lax.all_gather(values, 'blk', axis=1, tiled=True)  321 us
    all_to_all x2, blocking collectives, attend(): lax.all_to_all(out_part, 'blk', split_axis=1, concat_axis=2, tiled=True)  42.8 us
    all_to_all x3, waiting for transfers between devices, attend(): lax.all_to_all(columns, 'blk', split_axis=1, concat_axis=2, tiled=True)  34.9 us
  transfers between devices with their start and end apart: 18, of which 18 were waited for; matrix products, arithmetic and copies ran while one was open for 2% of the time, Pallas kernels for 0%

commit v1 on v0

--- a/solution.py
+++ b/solution.py
@@ -35,8 +35,11 @@
     q_heads = queries.reshape(num_req, num_rows, num_heads, 64)
     live_float = live.astype(jnp.float32)
     run_max = jnp.full((num_req, num_heads, num_rows), -1e30, jnp.float32)
-    key_piece = lax.all_gather(keys, "blk", axis=1, tiled=True)
-    value_piece = lax.all_gather(values, "blk", axis=1, tiled=True)
+    key_piece, value_piece = jnp.split(
+        lax.all_gather(jnp.concatenate([keys, values], 0), "blk", axis=1, tiled=True),
+        [keys.shape[0]],
+        0,
+    )
     piece_rows = key_piece.shape[1]
     key_heads = key_piece.reshape(num_req, piece_rows, num_heads, 64)
     value_heads = value_piece.reshape(num_req, piece_rows, num_heads, 64)

time: 1600 us -> 1320 us (0.82)
  waiting for transfers between devices: 1380 us -> 1070 us
  local copies, waits for them, and re-layouts: 72.8 us -> 103 us
    all_gather x6 -> x3, waiting for transfers between devices: 651 us -> 332 us  [attend(): lax.all_gather(jnp.concatenate([keys, values], 0), 'blk', axis=1, tiled=T...]
    split x0 -> x9, local copies, waits for them, and re-layouts: none -> 92.2 us  [attend(): jnp.split(lax.all_gather(jnp.concatenate([keys, values], 0), 'blk', axis=...]
    all_gather x6 -> x0, local copies, waits for them, and re-layouts: 59.8 us -> none  [the longest x3 29.9 us: attend(): key_piece = lax.all_gather(keys, 'blk', axis=1, tiled=True)]
  transfers between devices with their start and end apart: 18 -> 15, of which waited for: 18 -> 15; matrix products, arithmetic and copies ran while one was open for 2% -> 0% of each run, Pallas kernels for 0% -> 0%
where the time goes in v1:
time: 1320 us; the launch traced here: 1310 us
  waiting for transfers between devices  1070 us (81%)
  local copies, waits for them, and re-layouts  103 us (8%)
  blocking collectives  42.8 us (3%)
  starting transfers between devices  39.3 us (3%)
  matrix products  31.9 us (2%)
  between operations  16.6 us (1%)
    all_gather x3, waiting for transfers between devices, attend(): lax.all_gather(attn, 'blk', axis=1, tiled=True)  343 us
    all_gather x3, waiting for transfers between devices, attend(): lax.all_gather(normed_b, 'blk', axis=1, tiled=True)  343 us
    all_gather x3, waiting for transfers between devices, attend(): lax.all_gather(jnp.concatenate([keys, values], 0), 'blk', axis=1, tiled=T...  332 us
    split x9, local copies, waits for them, and re-layouts, attend(): jnp.split(lax.all_gather(jnp.concatenate([keys, values], 0), 'blk', axis=...  92.2 us
    all_to_all x2, blocking collectives, attend(): lax.all_to_all(out_part, 'blk', split_axis=1, concat_axis=2, tiled=True)  42.8 us
    all_to_all x3, waiting for transfers between devices, attend(): lax.all_to_all(columns, 'blk', split_axis=1, concat_axis=2, tiled=True)  34.8 us
    all_to_all x3, starting transfers between devices, attend(): lax.all_to_all(columns, 'blk', split_axis=1, concat_axis=2, tiled=True)  27.2 us
  transfers between devices with their start and end apart: 15, of which 15 were waited for; matrix products, arithmetic and copies ran while one was open for 0% of the time, Pallas kernels for 0%

profile of v1, /device:TPU:2, one launch (start us, length us, event | category | flops | bytes accessed | tf_op | source)
XLA Modules:
  0.0 1309.0 jit_solution(4533474868222683579)
XLA Ops:
  6.6 1.0 fusion.114
  7.6 1.0 multiply_reduce_fusion.2
  9.2 2.4 fusion.18
  11.7 0.7 add_convert_fusion.5
  12.8 120.3 %all-gather.10.cloned.1.call-done = bf16[1,384,3072]{2,0,1:T(2,128)(2,1)} async-done(((bf16[1,3,3072]{2,0,1:T(2,128)(2,1)}), bf16[1,384,3072]{2,0,1:T(2,128)(2,1)}) %all-gather.10.cloned.1.call-update) | async-done | bytes 2359312 | tf_op jit(solution)/shard_map/all_gather | solution.py:21
  133.0 3.2 fusion.42
  136.3 0.9 copy.107
  137.1 9.1 all-to-all-start
  146.4 0.7 fusion.124
  147.7 11.0 all-to-all-done
  158.7 0.6 reduce.19
  159.7 0.6 copy.109
  160.8 110.7 %all-gather.12.cloned.1.call-done = bf16[2,384,3072]{2,0,1:T(2,128)(2,1)} async-done(((bf16[2,3,3072]{2,0,1:T(2,128)(2,1)}), bf16[2,384,3072]{2,0,1:T(2,128)(2,1)}) %all-gather.12.cloned.1.call-update) | async-done | bytes 4718608 | tf_op jit(solution)/shard_map/all_gather | solution.py:39
  271.5 10.8 fusion.119
  282.3 10.0 copy.110
  292.3 0.6 fusion.125
  292.9 10.0 copy.112
  303.1 2.6 fusion.47
  305.8 0.7 convert_element_type.264
  306.6 114.2 %all-gather.14.cloned.1.call-done = bf16[1,384,3072]{2,0,1:T(2,128)(2,1)} async-done(((bf16[1,3,3072]{2,0,1:T(2,128)(2,1)}), bf16[1,384,3072]{2,0,1:T(2,128)(2,1)}) %all-gather.14.cloned.1.call-update) | async-done | bytes 2359312 | tf_op jit(solution)/shard_map/all_gather | solution.py:65
  420.7 3.1 fusion.63
  424.0 21.4 %all_to_all.81 = bf16[1,384,24]{2,0,1:T(2,128)(2,1)S(1)} all-to-all(bf16[1,384,24]{2,0,1:T(2,128)(2,1)S(1)} %copy.115), channel_id=1, replica_groups=mesh['section'=2,'blk'=128] {'blk'}, dimensions={1} | all-to-all | bytes 36864 | tf_op jit(solution)/shard_map/all_to_all | solution.py:69
  445.9 1.3 collective-permute-start
  447.2 0.8 collective-permute-done
  448.5 0.7 add_convert_fusion.3
  449.2 111.1 %all-gather.16.cloned.1.call-done = bf16[1,384,3072]{2,0,1:T(2,128)(2,1)} async-done(((bf16[1,3,3072]{2,0,1:T(2,128)(2,1)}), bf16[1,384,3072]{2,0,1:T(2,128)(2,1)}) %all-gather.16.cloned.1.call-update) | async-done | bytes 2359312 | tf_op jit(solution)/shard_map/all_gather | solution.py:21
  560.4 3.2 fusion.39
  563.6 0.8 copy.117
  564.5 9.1 all-to-all-start.2
  574.2 11.9 all-to-all-done.2
  586.1 0.6 reduce.21
  587.0 0.6 copy.119
  588.1 110.7 %all-gather.18.cloned.1.call-done = bf16[2,384,3072]{2,0,1:T(2,128)(2,1)} async-done(((bf16[2,3,3072]{2,0,1:T(2,128)(2,1)}), bf16[2,384,3072]{2,0,1:T(2,128)(2,1)}) %all-gather.18.cloned.1.call-update) | async-done | bytes 4718608 | tf_op jit(solution)/shard_map/all_gather | solution.py:39
  698.8 10.8 fusion.118
  709.7 10.0 copy.120
  719.6 0.6 fusion.126
  720.2 10.0 copy.122
  730.5 2.6 fusion.46
  733.1 0.7 convert_element_type.265
  733.9 114.2 %all-gather.20.cloned.1.call-done = bf16[1,384,3072]{2,0,1:T(2,128)(2,1)} async-done(((bf16[1,3,3072]{2,0,1:T(2,128)(2,1)}), bf16[1,384,3072]{2,0,1:T(2,128)(2,1)}) %all-gather.20.cloned.1.call-update) | async-done | bytes 2359312 | tf_op jit(solution)/shard_map/all_gather | solution.py:65
  848.1 3.1 fusion.60
  851.4 21.4 %all_to_all.82 = bf16[1,384,24]{2,0,1:T(2,128)(2,1)S(1)} all-to-all(bf16[1,384,24]{2,0,1:T(2,128)(2,1)S(1)} %copy.125), channel_id=1, replica_groups=mesh['section'=2,'blk'=128] {'blk'}, dimensions={1} | all-to-all | bytes 36864 | tf_op jit(solution)/shard_map/all_to_all | solution.py:69
  873.2 1.3 collective-permute-start.1
  874.5 0.8 collective-permute-done.1
  875.7 0.7 add_convert_fusion.1
  876.5 111.1 %all-gather.22.cloned.1.call-done = bf16[1,384,3072]{2,0,1:T(2,128)(2,1)} async-done(((bf16[1,3,3072]{2,0,1:T(2,128)(2,1)}), bf16[1,384,3072]{2,0,1:T(2,128)(2,1)}) %all-gather.22.cloned.1.call-update) | async-done | bytes 2359312 | tf_op jit(solution)/shard_map/all_gather | solution.py:21
  987.6 3.2 fusion.36
  990.9 0.8 copy.127
  991.7 9.1 all-to-all-start.4
  1001.5 11.8 all-to-all-done.4
  1014.3 0.6 copy.129
  1015.4 110.7 %all-gather.24.cloned.1.call-done = bf16[2,384,3072]{2,0,1:T(2,128)(2,1)} async-done(((bf16[2,3,3072]{2,0,1:T(2,128)(2,1)}), bf16[2,384,3072]{2,0,1:T(2,128)(2,1)}) %all-gather.24.cloned.1.call-update) | async-done | bytes 4718608 | tf_op jit(solution)/shard_map/all_gather | solution.py:39
  1126.1 10.8 fusion.117
  1136.9 10.0 copy.130
  1146.9 0.6 fusion.127
  1147.5 10.0 copy.132
  1157.7 2.6 fusion.45
  1160.4 0.7 convert_element_type.266
  1161.1 114.2 %all-gather.26.cloned.1.call-done = bf16[1,384,3072]{2,0,1:T(2,128)(2,1)} async-done(((bf16[1,3,3072]{2,0,1:T(2,128)(2,1)}), bf16[1,384,3072]{2,0,1:T(2,128)(2,1)}) %all-gather.26.cloned.1.call-update) | async-done | bytes 2359312 | tf_op jit(solution)/shard_map/all_gather | solution.py:65
  1275.3 3.1 fusion.57
  1278.4 0.9 copy.135
  1279.3 9.1 all-to-all-start.5
  1288.4 12.5 all-to-all-done.5
  1301.4 0.6 copy.137
  (100 shorter events, 7.0 us)
Async XLA Ops:
  6.5 126.5 %copy-start = (bf16[1,3072,72]{1,2,0:T(8,128)(2,1)S(1)}, bf16[1,3072,72]{1,2,0:T(8,128)(2,1)}, u32[]{:S(2)}) copy-start(bf16[1,3072,72]{1,2,0:T(8,128)(2,1)} %param.10) | copy-start | bytes 1327108
  6.5 5.1 copy-start.1
  6.5 6.0 copy-start.3
  6.5 6.0 copy-start.2
  6.5 126.5 %all-gather.10.cloned.1.call-start = ((), (), s32[]{:S(2)}) async-start(), calls=%async_computation.6 | async-start | bytes 4755456 | tf_op jit(solution)/shard_map/all_gather | solution.py:21
  12.5 133.8 %copy-start.4 = (s32[1,2,128]{2,1,0:T(2,128)S(1)}, s32[1,2,128]{2,1,0:T(2,128)}, u32[]{:S(2)}) copy-start(s32[1,2,128]{2,1,0:T(2,128)} %param.14) | copy-start | bytes 3076
  12.8 147.7 %copy-start.6 = (s32[2,128]{1,0:T(2,128)S(1)}, s32[2,128]{1,0:T(2,128)}, u32[]{:S(2)}) copy-start(s32[2,128]{1,0:T(2,128)} %param.15) | copy-start | bytes 3076
  137.1 21.6 %all-to-all-start = ((bf16[1,384,72]{2,0,1:T(2,128)(2,1)}), bf16[1,384,72]{2,0,1:T(2,128)(2,1)S(1)}, u32[]{:S(2)}, u32[]{:S(2)}) async-start(bf16[1,384,72]{2,0,1:T(2,128)(2,1)} %copy.107), calls=%async_computation | async-start | bytes 393216 | tf_op jit(solution)/shard_map/all_to_all | solution.py:25
  146.2 125.3 %all-gather.12.cloned.1.call-start = ((), (), s32[]{:S(2)}) async-start(), calls=%async_computation.7 | async-start | bytes 4755456 | tf_op jit(solution)/shard_map/all_gather | solution.py:39
  160.4 260.4 %all-gather.14.cloned.1.call-start = ((), (), s32[]{:S(2)}) async-start(), calls=%async_computation.8 | async-start | bytes 4755456 | tf_op jit(solution)/shard_map/all_gather | solution.py:65
  302.9 117.9 %copy-start.5 = (bf16[1,3072,24]{1,2,0:T(8,128)(2,1)S(1)}, bf16[1,3072,24]{1,2,0:T(8,128)(2,1)}, u32[]{:S(2)}) copy-start(bf16[1,3072,24]{1,2,0:T(8,128)(2,1)} %param.11) | copy-start | bytes 442372
  306.5 253.9 %all-gather.16.cloned.1.call-start = ((), (), s32[]{:S(2)}) async-start(), calls=%async_computation.9 | async-start | bytes 4755456 | tf_op jit(solution)/shard_map/all_gather | solution.py:21
  445.9 2.1 collective-permute-start
  564.5 21.6 %all-to-all-start.2 = ((bf16[1,384,72]{2,0,1:T(2,128)(2,1)}), bf16[1,384,72]{2,0,1:T(2,128)(2,1)S(1)}, u32[]{:S(2)}, u32[]{:S(2)}) async-start(bf16[1,384,72]{2,0,1:T(2,128)(2,1)} %copy.117), calls=%async_computation.2 | async-start | bytes 393216 | tf_op jit(solution)/shard_map/all_to_all | solution.py:25
  573.5 125.3 %all-gather.18.cloned.1.call-start = ((), (), s32[]{:S(2)}) async-start(), calls=%async_computation.10 | async-start | bytes 4755456 | tf_op jit(solution)/shard_map/all_gather | solution.py:39
  587.7 260.3 %all-gather.20.cloned.1.call-start = ((), (), s32[]{:S(2)}) async-start(), calls=%async_computation.11 | async-start | bytes 4755456 | tf_op jit(solution)/shard_map/all_gather | solution.py:65
  733.8 253.8 %all-gather.22.cloned.1.call-start = ((), (), s32[]{:S(2)}) async-start(), calls=%async_computation.12 | async-start | bytes 4755456 | tf_op jit(solution)/shard_map/all_gather | solution.py:21
  873.2 2.1 collective-permute-start.1
  991.7 21.6 %all-to-all-start.4 = ((bf16[1,384,72]{2,0,1:T(2,128)(2,1)}), bf16[1,384,72]{2,0,1:T(2,128)(2,1)S(1)}, u32[]{:S(2)}, u32[]{:S(2)}) async-start(bf16[1,384,72]{2,0,1:T(2,128)(2,1)} %copy.127), calls=%async_computation.4 | async-start | bytes 393216 | tf_op jit(solution)/shard_map/all_to_all | solution.py:25
  1000.8 125.3 %all-gather.24.cloned.1.call-start = ((), (), s32[]{:S(2)}) async-start(), calls=%async_computation.13 | async-start | bytes 4755456 | tf_op jit(solution)/shard_map/all_gather | solution.py:39
  1015.0 260.3 %all-gather.26.cloned.1.call-start = ((), (), s32[]{:S(2)}) async-start(), calls=%async_computation.14 | async-start | bytes 4755456 | tf_op jit(solution)/shard_map/all_gather | solution.py:65
  1279.3 21.6 %all-to-all-start.5 = ((bf16[1,384,24]{2,0,1:T(2,128)(2,1)}), bf16[1,384,24]{2,0,1:T(2,128)(2,1)S(1)}, u32[]{:S(2)}, u32[]{:S(2)}) async-start(bf16[1,384,24]{2,0,1:T(2,128)(2,1)} %copy.135), calls=%async_computation.5 | async-start | bytes 393216 | tf_op jit(solution)/shard_map/all_to_all | solution.py:69
Sparse Core Ops, SparseCore 0:
  12.6 120.4 all-gather.9
  160.5 110.9 all-gather.11
  306.6 114.0 all-gather.13
  449.4 110.9 all-gather.15
  587.8 110.9 all-gather.17
  733.9 114.0 all-gather.19
  876.6 110.9 all-gather.21
  1015.1 110.9 all-gather.23
  1161.2 114.0 all-gather.25
